TPU v7x, 128 devices: a whole 4x4x4 slice. The times are simulated.
128 devices in a mesh: section: 2 (over x_lo), expert: 16 (over z, x_hi, core), dp: 4 (over y).
Axes of the slice: x: 4 (x_hi: 2, x_lo: 2; x = x_hi * 2 + x_lo), y: 4, z: 4, core: 2. Of those that a mesh axis runs over, the one named last changes fastest.
Arguments:
- fresh_tokens: bfloat16 [2, 4096, 4096], P(None, ('expert', 'dp')), may hold values from -60 to 60
- in_flight: bfloat16 [4096, 4096], P(('expert', 'dp')), may hold values from -60 to 60
- norm_weight: float32 [2, 4096], P('section'), may hold values from 0.1 to 1.9
- gate_up: bfloat16 [2, 16, 2, 4096, 768], P('section', 'expert', None, 'dp'), may hold values from -0.09375 to 0.09375
- down_proj: bfloat16 [2, 16, 768, 4096], P('section', 'expert', 'dp'), may hold values from -0.21875 to 0.21875
- first_moment: bfloat16 [2, 16, 768, 4096], P('section', 'expert', 'dp'), may hold values from -6 to 6
- second_moment: bfloat16 [2, 16, 768, 4096], P('section', 'expert', 'dp'), may hold values from 0.099609375 to 4
- route_ids: int32 [2, 2, 4096, 8], P('section', None, ('expert', 'dp')), may hold values from 0 to 15, all different within a row; in each aligned block of 64 rows (0 to 63, 64 to 127, ..., all dimensions but the last counted through in order) at most 36 rows name the same one
- route_probs: float32 [2, 2, 4096, 8], P('section', None, ('expert', 'dp')), may hold values from 0.05 to 1
- trade_flags: int32 [8, 1], replicated, may hold values from 0 to 1, as said below
Outputs:
- layer_out: bfloat16 [2, 2, 4096, 4096], P('section', None, ('expert', 'dp'))
- gate_up_moved: bfloat16 [2, 16, 2, 4096, 768], P('section', 'expert', None, 'dp')
- down_moved: bfloat16 [2, 16, 768, 4096], P('section', 'expert', 'dp')
- first_moved: bfloat16 [2, 16, 768, 4096], P('section', 'expert', 'dp')
- second_moved: bfloat16 [2, 16, 768, 4096], P('section', 'expert', 'dp')
Inputs may be any that keep to these rules, and one draw needn't show every extreme that they name: `route_ids`: in each aligned block of 64 rows (one device's tokens of one section and tick) the 8 experts of a token differ and no expert is chosen by more than 36 rows. `trade_flags`: at least one entry is 1 and at least one is 0.
All inputs are finite; a program needn't handle non-finite values.
Results may differ from a plain program's by a relative error of at most 0.0035.
Values may be sent and summed in bfloat16 or wider, within the bound.
A program may use at most 128 MiB of HBM per device.

v0:
```python
import jax
import jax.numpy as jnp
from jax import lax
from jax.sharding import PartitionSpec as P

EXPERTS = 16


def partner(value, axis, bit):
    return lax.ppermute(value, axis, [(i, i ^ 1 << bit) for i in range(lax.axis_size(axis))])


def shifted(block, axis, distance):
    devices = range(lax.axis_size(axis))
    route = [(i - distance, i) for i in devices if i - distance in devices]
    return lax.ppermute(block, axis, route)


def rms_normed(inputs, norm_gain):
    values = inputs.astype(jnp.float32)
    inverse_rms = lax.rsqrt(jnp.mean(values * values, axis=-1, keepdims=True) + 1e-06)
    return (values * inverse_rms * norm_gain).astype(jnp.bfloat16)


def per_device(
    fresh_tokens,
    in_flight,
    norm_weight,
    gate_up,
    down_proj,
    first_moment,
    second_moment,
    route_ids,
    route_probs,
    trade_flags,
):
    groups = lax.axis_size("expert")
    half_span = groups // 2
    top_bit = groups.bit_length() - 2
    own_rank = lax.axis_index("expert")
    section_index = lax.axis_index("section")
    full_gate_up = lax.all_gather(gate_up, "dp", axis=3, tiled=True)
    full_down = lax.all_gather(down_proj, "dp", axis=2, tiled=True)
    gate_weights = full_gate_up[0, 0, 0]
    up_weights = full_gate_up[0, 0, 1]
    down_weights = full_down[0, 0]
    expert_ids = jnp.arange(EXPERTS, dtype=jnp.int32)
    probs = route_probs[0]
    mix = probs / jnp.sum(probs, axis=-1, keepdims=True)
    chosen = route_ids[0][:, :, :, None] == expert_ids
    dense_mix = jnp.sum(jnp.where(chosen, mix[:, :, :, None], 0.0), axis=2)
    all_mix = lax.all_gather(dense_mix, "expert", axis=1, tiled=True)
    own_mix = jnp.sum(jnp.where(expert_ids == own_rank, all_mix, 0.0), axis=-1)
    traded = partner((gate_up, down_proj, first_moment, second_moment), "expert", top_bit)

    def layer(inputs, scale, held=None):
        normed = rms_normed(inputs, norm_weight[0])
        arrived = lax.all_gather(normed, "expert", axis=0, tiled=True)
        gate_part = jnp.dot(arrived, gate_weights, preferred_element_type=jnp.float32)
        up_part = jnp.dot(arrived, up_weights, preferred_element_type=jnp.float32)
        active = (jax.nn.silu(gate_part) * up_part).astype(jnp.bfloat16)
        result = jnp.dot(active, down_weights, preferred_element_type=jnp.float32)
        result = (result * scale[:, None]).astype(jnp.bfloat16)
        if held is not None:
            result, held = lax.optimization_barrier((result, held))
        combined = lax.psum_scatter(result, "expert", scatter_dimension=0, tiled=True)
        return (
            (inputs.astype(jnp.float32) + combined.astype(jnp.float32)).astype(jnp.bfloat16),
            held,
        )

    first_input = jnp.where(section_index == 0, fresh_tokens[0], in_flight)
    tick_zero, traded = layer(first_input, own_mix[0], traded)
    arrived = shifted(tick_zero, "section", 1)
    second_input = jnp.where(section_index == 0, fresh_tokens[1], arrived)
    tick_one, _ = layer(second_input, own_mix[1])
    layer_out = jnp.stack([tick_zero, tick_one])[None]
    own_flags = trade_flags[own_rank % half_span] == 1
    mask_five = own_flags[None, :, None, None, None]
    mask_four = own_flags[None, :, None, None]
    gate_up_moved = jnp.where(mask_five, traded[0], gate_up)
    down_moved = jnp.where(mask_four, traded[1], down_proj)
    first_moved = jnp.where(mask_four, traded[2], first_moment)
    second_moved = jnp.where(mask_four, traded[3], second_moment)
    return (layer_out, gate_up_moved, down_moved, first_moved, second_moved)


def solution(mesh):
    return jax.shard_map(
        per_device,
        mesh=mesh,
        in_specs=(
            P(None, ("expert", "dp"), None),
            P(("expert", "dp"), None),
            P("section", None),
            P("section", "expert", None, "dp", None),
            P("section", "expert", "dp", None),
            P("section", "expert", "dp", None),
            P("section", "expert", "dp", None),
            P("section", None, ("expert", "dp"), None),
            P("section", None, ("expert", "dp"), None),
            P(),
        ),
        out_specs=(
            P("section", None, ("expert", "dp"), None),
            P("section", "expert", None, "dp", None),
            P("section", "expert", "dp", None),
            P("section", "expert", "dp", None),
            P("section", "expert", "dp", None),
        ),
        check_vma=False,
    )
```

profile of v0, /device:TPU:0, one launch (start us, length us, event | category | flops | bytes accessed | tf_op | source)
XLA Modules:
  0.0 780.1 jit_solution(14578231850789856475)
XLA Ops:
  7.2 1.3 fusion.6
  9.4 1.8 fusion.8
  12.8 4.0 collective-permute-start.1
  16.9 3.4 collective-permute-start.2
  20.6 35.1 %all_gather.18 = f32[2,1024,16]{2,0,1:T(2,128)S(1)} all-gather(f32[2,64,16]{2,0,1:T(2,128)S(1)} %copy.17), channel_id=1, replica_groups=mesh['section'=2,'expert'=16,'dp'=4] {'expert'}, dimensions={1}, use_global_device_ids=true | all-gather | bytes 139264 | tf_op jit(solution)/shard_map/all_gather | solution.py:52
  59.2 187.8 %all-gather.5.cloned.1.call-done = bf16[1024,4096]{1,0:T(8,128)(2,1)} async-done(((bf16[64,4096]{1,0:T(8,128)(2,1)}), bf16[1024,4096]{1,0:T(8,128)(2,1)}) %all-gather.5.cloned.1.call-update) | async-done | bytes 8388624 | tf_op jit(solution)/shard_map/all_gather | solution.py:58
  247.0 118.0 %all-gather.7.cloned.1.call-done = bf16[1,1,2,4096,768]{4,3,2,1,0:T(8,128)(2,1)} async-done(((bf16[1,1,2,1024,768]{4,3,2,1,0:T(8,128)(2,1)}), bf16[1,1,2,4096,768]{4,3,2,1,0:T(8,128)(2,1)}) %all-gather.7.cloned.1.call-update) | async-done | bytes 12582928 | tf_op jit(solution)/shard_map/all_gather | solution.py:42
  365.0 11.0 %fusion.5 = f32[1024,768]{1,0:T(8,128)S(1)} fusion(bf16[1024,4096]{1,0:T(8,128)(2,1)} %all-gather.5.cloned.1.call-done, bf16[1,1,2,4096,768]{4,3,2,1,0:T(8,128)(2,1)} %all-gather.7.cloned.1.call-done), kind=kOutput, calls=%fused_computation.9 | convolution fusion | flops 6442450944 | bytes 17825792 | tf_op jit(solution)/shard_map/dot_general | solution.py:60
  376.2 8.1 %multiply_convert_fusion.3 = bf16[1024,768]{1,0:T(8,128)(2,1)} fusion(f32[1024,768]{1,0:T(8,128)S(1)} %fusion.5, bf16[1024,4096]{1,0:T(8,128)(2,1)S(1)} %copy-done.13, bf16[1,1,2,4096,768]{4,3,2,1,0:T(8,128)(2,1)S(1)} %copy-done.12), kind=kOutput, calls=%fused_computation.11 | convolution fusion | flops 6447169536 | bytes 19398656 | tf_op jit(solution)/shard_map/dot_general | solution.py:59
  384.2 49.1 %all-gather.9.cloned.1.call-done = bf16[1,1,768,4096]{3,2,1,0:T(8,128)(2,1)} async-done(((bf16[1,1,192,4096]{3,2,1,0:T(8,128)(2,1)}), bf16[1,1,768,4096]{3,2,1,0:T(8,128)(2,1)}) %all-gather.9.cloned.1.call-update) | async-done | bytes 6291472 | tf_op jit(solution)/shard_map/all_gather | solution.py:43
  433.4 11.2 %multiply_convert_fusion.1 = bf16[1024,4096]{1,0:T(8,128)(2,1)} fusion(f32[1024]{0:T(1024)S(1)} %bitcast.45, bf16[1024,768]{1,0:T(8,128)(2,1)} %multiply_convert_fusion.3, bf16[1,1,768,4096]{3,2,1,0:T(8,128)(2,1)} %all-gather.9.cloned.1.call-done), kind=kOutput, calls=%fused_computation.1 | convolution fusion | flops 6450839552 | bytes 16257024 | tf_op jit(solution)/shard_map/dot_general | solution.py:62
  444.7 103.2 %reduce-scatter.3.cloned.1.call-done = bf16[64,4096]{1,0:T(8,128)(2,1)} async-done(((bf16[1024,4096]{1,0:T(8,128)(2,1)}), bf16[64,4096]{1,0:T(8,128)(2,1)}) %reduce-scatter.3.cloned.1.call-update) | async-done | bytes 524304 | tf_op jit(solution)/shard_map/reduce_scatter | solution.py:66
  547.9 1.3 fusion.9
  549.3 2.5 collective-permute-start.4
  551.8 10.1 %collective-permute-done.4 = bf16[64,4096]{1,0:T(8,128)(2,1)S(1)} collective-permute-done((bf16[64,4096]{1,0:T(8,128)(2,1)S(1)}, bf16[64,4096]{1,0:T(8,128)(2,1)S(1)}, u32[]{:S(2)}, u32[]{:S(2)}) %collective-permute-start.4) | collective-permute-done | bytes 524320 | tf_op jit(solution)/shard_map/ppermute | solution.py:16
  561.9 1.3 fusion.10
  566.5 71.6 %all-gather.11.cloned.1.call-done = bf16[1024,4096]{1,0:T(8,128)(2,1)} async-done(((bf16[64,4096]{1,0:T(8,128)(2,1)}), bf16[1024,4096]{1,0:T(8,128)(2,1)}) %all-gather.11.cloned.1.call-update) | async-done | bytes 8388624 | tf_op jit(solution)/shard_map/all_gather | solution.py:58
  638.1 11.0 %fusion.4 = f32[1024,768]{1,0:T(8,128)S(1)} fusion(bf16[1024,4096]{1,0:T(8,128)(2,1)} %all-gather.11.cloned.1.call-done, bf16[1,1,2,4096,768]{4,3,2,1,0:T(8,128)(2,1)} %all-gather.7.cloned.1.call-done), kind=kOutput, calls=%fused_computation.8 | convolution fusion | flops 6442450944 | bytes 17825792 | tf_op jit(solution)/shard_map/dot_general | solution.py:60
  649.1 9.8 %multiply_convert_fusion.2 = bf16[1024,768]{1,0:T(8,128)(2,1)S(1)} fusion(f32[1024,768]{1,0:T(8,128)S(1)} %fusion.4, bf16[1024,4096]{1,0:T(8,128)(2,1)S(1)} %copy-done.14, bf16[1,1,2,4096,768]{4,3,2,1,0:T(8,128)(2,1)} %all-gather.7.cloned.1.call-done), kind=kOutput, calls=%fused_computation.10 | convolution fusion | flops 6447169536 | bytes 19398656 | tf_op jit(solution)/shard_map/dot_general | solution.py:59
  658.9 11.7 %multiply_convert_fusion = bf16[1024,4096]{1,0:T(8,128)(2,1)} fusion(f32[1024]{0:T(1024)S(1)} %bitcast.46, bf16[1024,768]{1,0:T(8,128)(2,1)S(1)} %multiply_convert_fusion.2, bf16[1,1,768,4096]{3,2,1,0:T(8,128)(2,1)} %all-gather.9.cloned.1.call-done), kind=kOutput, calls=%fused_computation | convolution fusion | flops 6450839552 | bytes 16257024 | tf_op jit(solution)/shard_map/dot_general | solution.py:62
  671.9 4.6 broadcast_select_fusion
  676.6 4.0 broadcast_select_fusion.3
  680.5 4.9 broadcast_select_fusion.1
  685.4 85.6 %reduce-scatter.5.cloned.1.call-done = bf16[64,4096]{1,0:T(8,128)(2,1)} async-done(((bf16[1024,4096]{1,0:T(8,128)(2,1)}), bf16[64,4096]{1,0:T(8,128)(2,1)}) %reduce-scatter.5.cloned.1.call-update) | async-done | bytes 524304 | tf_op jit(solution)/shard_map/reduce_scatter | solution.py:66
  (65 shorter events, 13.2 us)
Async XLA Ops:
  7.2 239.8 %all-gather.5.cloned.1.call-start = ((), (), s32[]{:S(2)}) async-start(), calls=%async_computation.2 | async-start | bytes 8912896 | tf_op jit(solution)/shard_map/all_gather | solution.py:58
  9.4 7.5 copy-start
  9.4 11.1 %copy-start.10 = (f32[1,2,64,8]{2,3,1,0:T(8,128)S(1)}, f32[1,2,64,8]{2,3,1,0:T(8,128)}, u32[]{:S(2)}) copy-start(f32[1,2,64,8]{2,3,1,0:T(8,128)} %param.18) | copy-start | bytes 12292
  9.4 11.1 %copy-start.11 = (s32[1,2,64,8]{2,3,1,0:T(8,128)S(1)}, s32[1,2,64,8]{2,3,1,0:T(8,128)}, u32[]{:S(2)}) copy-start(s32[1,2,64,8]{2,3,1,0:T(8,128)} %param.17) | copy-start | bytes 12292
  11.2 353.7 %all-gather.7.cloned.1.call-start = ((), (), s32[]{:S(2)}) async-start(), calls=%async_computation.3 | async-start | bytes 15728640 | tf_op jit(solution)/shard_map/all_gather | solution.py:42
  12.0 421.4 %all-gather.9.cloned.1.call-start = ((), (), s32[]{:S(2)}) async-start(), calls=%async_computation.4 | async-start | bytes 7864320 | tf_op jit(solution)/shard_map/all_gather | solution.py:43
  12.7 535.2 %reduce-scatter.3.cloned.1.call-start = ((), (), s32[]{:S(2)}) async-start(), calls=%async_computation.5 | async-start | bytes 8912896 | tf_op jit(solution)/shard_map/reduce_scatter | solution.py:66
  12.8 431.9 %collective-permute-start.1 = (bf16[1,1,192,4096]{3,2,1,0:T(8,128)(2,1)}, bf16[1,1,192,4096]{3,2,1,0:T(8,128)(2,1)}, u32[]{:S(2)}, u32[]{:S(2)}) collective-permute-start(bf16[1,1,192,4096]{3,2,1,0:T(8,128)(2,1)} %param.14), channel_id=1, source_target_pairs={{0,32},{4,36},{8,40},{12,44},{16,48},{20,52},{24,56},{28,60},{32,0... | collective-permute-start | bytes 4718600 | tf_op jit(solution)/shard_map/ppermute | solution.py:10
  16.8 427.8 %collective-permute-start = (bf16[1,1,2,1024,768]{4,3,2,1,0:T(8,128)(2,1)S(1)}, bf16[1,1,2,1024,768]{4,3,2,1,0:T(8,128)(2,1)}, u32[]{:S(2)}, u32[]{:S(2)}) collective-permute-start(bf16[1,1,2,1024,768]{4,3,2,1,0:T(8,128)(2,1)S(1)} %copy-done), channel_id=1, source_target_pairs={{0,32},{4,36},{8,40},{12,44},{16,48},{20,52},{24,56},{28,60},{32,0... | collective-permute-start | bytes 9437192 | tf_op jit(solution)/shard_map/ppermute | solution.py:10
  16.9 427.7 %collective-permute-start.2 = (bf16[1,1,192,4096]{3,2,1,0:T(8,128)(2,1)}, bf16[1,1,192,4096]{3,2,1,0:T(8,128)(2,1)}, u32[]{:S(2)}, u32[]{:S(2)}) collective-permute-start(bf16[1,1,192,4096]{3,2,1,0:T(8,128)(2,1)} %param.15), channel_id=1, source_target_pairs={{0,32},{4,36},{8,40},{12,44},{16,48},{20,52},{24,56},{28,60},{32,0... | collective-permute-start | bytes 4718600 | tf_op jit(solution)/shard_map/ppermute | solution.py:10
  20.3 424.3 %collective-permute-start.3 = (bf16[1,1,192,4096]{3,2,1,0:T(8,128)(2,1)}, bf16[1,1,192,4096]{3,2,1,0:T(8,128)(2,1)}, u32[]{:S(2)}, u32[]{:S(2)}) collective-permute-start(bf16[1,1,192,4096]{3,2,1,0:T(8,128)(2,1)} %param.16), channel_id=1, source_target_pairs={{0,32},{4,36},{8,40},{12,44},{16,48},{20,52},{24,56},{28,60},{32,0... | collective-permute-start | bytes 4718600 | tf_op jit(solution)/shard_map/ppermute | solution.py:10
  365.0 11.0 %copy-start.12 = (bf16[1,1,2,4096,768]{4,3,2,1,0:T(8,128)(2,1)S(1)}, bf16[1,1,2,4096,768]{4,3,2,1,0:T(8,128)(2,1)}, u32[]{:S(2)}) copy-start(bf16[1,1,2,4096,768]{4,3,2,1,0:T(8,128)(2,1)} %all-gather.7.cloned.1.call-done) | copy-start | bytes 37748740
  365.0 11.2 %copy-start.13 = (bf16[1024,4096]{1,0:T(8,128)(2,1)S(1)}, bf16[1024,4096]{1,0:T(8,128)(2,1)}, u32[]{:S(2)}) copy-start(bf16[1024,4096]{1,0:T(8,128)(2,1)} %all-gather.5.cloned.1.call-done) | copy-start | bytes 25165828
  444.7 119.3 %copy-start.9 = (f32[1,4096]{1,0:T(1,128)S(1)}, f32[1,4096]{1,0:T(1,128)}, u32[]{:S(2)}) copy-start(f32[1,4096]{1,0:T(1,128)} %param.12) | copy-start | bytes 49156
  444.7 193.4 %all-gather.11.cloned.1.call-start = ((), (), s32[]{:S(2)}) async-start(), calls=%async_computation.6 | async-start | bytes 8912896 | tf_op jit(solution)/shard_map/all_gather | solution.py:58
  549.3 2.5 copy-start.5
  549.3 12.6 %collective-permute-start.4 = (bf16[64,4096]{1,0:T(8,128)(2,1)S(1)}, bf16[64,4096]{1,0:T(8,128)(2,1)S(1)}, u32[]{:S(2)}, u32[]{:S(2)}) collective-permute-start(bf16[64,4096]{1,0:T(8,128)(2,1)S(1)} %fusion.9), channel_id=1, source_target_pairs={{0,64},{1,65},{2,66},{3,67},{4,68},{5,69},{6,70},{7,71},{8,72},{9,... | collective-permute-start | bytes 1572872 | tf_op jit(solution)/shard_map/ppermute | solution.py:16
  565.0 206.0 %reduce-scatter.5.cloned.1.call-start = ((), (), s32[]{:S(2)}) async-start(), calls=%async_computation.7 | async-start | bytes 8912896 | tf_op jit(solution)/shard_map/reduce_scatter | solution.py:66
  638.1 11.1 %copy-start.14 = (bf16[1024,4096]{1,0:T(8,128)(2,1)S(1)}, bf16[1024,4096]{1,0:T(8,128)(2,1)}, u32[]{:S(2)}) copy-start(bf16[1024,4096]{1,0:T(8,128)(2,1)} %all-gather.11.cloned.1.call-done) | copy-start | bytes 25165828
  671.9 4.7 copy-start.1
  676.6 4.0 copy-start.7
  676.6 4.0 copy-start.8
  680.5 90.5 %copy-start.4 = (bf16[64,4096]{1,0:T(8,128)(2,1)S(1)}, bf16[64,4096]{1,0:T(8,128)(2,1)}, u32[]{:S(2)}) copy-start(bf16[64,4096]{1,0:T(8,128)(2,1)} %copy-done.3) | copy-start | bytes 1572868
  680.5 91.6 %copy-start.6 = (bf16[64,4096]{1,0:T(8,128)(2,1)S(1)}, bf16[64,4096]{1,0:T(8,128)(2,1)}, u32[]{:S(2)}) copy-start(bf16[64,4096]{1,0:T(8,128)(2,1)} %copy-done.5) | copy-start | bytes 1572868
  (3 other events, 2.3 us)
Sparse Core Ops, SparseCore 0:
  11.4 235.5 all-gather.4
  248.6 116.2 all-gather.6
  366.6 66.6 all-gather.8
  444.8 103.1 reduce-scatter.2
  565.1 72.8 all-gather.10
  670.8 100.1 reduce-scatter.4
where the time goes:
time: 781 us; the launch traced here: 780 us
  waiting for transfers between devices  627 us (80%)
  matrix products  62.9 us (8%)
  blocking collectives  35.1 us (4%)
  other arithmetic  24.4 us (3%)
  between operations  14.3 us (2%)
  starting transfers between devices  10.6 us (1%)
    all_gather x2, waiting for transfers between devices, layer(): arrived = lax.all_gather(normed, 'expert', axis=0, tiled=True)  259 us
    reduce_scatter x2, waiting for transfers between devices, layer(): lax.psum_scatter(result, 'expert', scatter_dimension=0, tiled=True)  189 us
    all_gather x1, waiting for transfers between devices, per_device(): full_gate_up = lax.all_gather(gate_up, 'dp', axis=3, tiled=True)  118 us
    all_gather x1, waiting for transfers between devices, per_device(): full_down = lax.all_gather(down_proj, 'dp', axis=2, tiled=True)  49.1 us
    all_gather x1, blocking collectives, per_device(): all_mix = lax.all_gather(dense_mix, 'expert', axis=1, tiled=True)  35.1 us
    dot_general x2, matrix products, layer(): result = jnp.dot(active, down_weights, preferred_element_type=jnp.float32)  23 us
    dot_general x2, matrix products, layer(): up_part = jnp.dot(arrived, up_weights, preferred_element_type=jnp.float32)  22.1 us
    dot_general x2, matrix products, layer(): jnp.dot(arrived, gate_weights, preferred_element_type=jnp.float32)  17.8 us
  transfers between devices with their start and end apart: 11, of which 7 were waited for; matrix products, arithmetic and copies ran while one was open for 6% of the time, Pallas kernels for 0%

commit v1 on v0

--- a/solution.py
+++ b/solution.py
@@ -4,6 +4,28 @@
 from jax.sharding import PartitionSpec as P
 
 EXPERTS = 16
+
+
+def laid_out(pieces, dim):
+    pieces = jnp.moveaxis(pieces, 0, dim)
+    shape = pieces.shape
+    return pieces.reshape(*shape[:dim], shape[dim] * shape[dim + 1], *shape[dim + 2 :])
+
+
+def collect(shard, axis, dim):
+    peers = lax.axis_size(axis)
+    pairs = [(i, (i + 1) % peers) for i in range(peers)]
+    back = [(b, a) for a, b in pairs]
+    lower, upper = ([], [])
+    for hop in range(peers - 1):
+        if hop % 2 == 0:
+            lower.append(lax.ppermute(lower[-1] if lower else shard, axis, pairs))
+        else:
+            upper.append(lax.ppermute(upper[-1] if upper else shard, axis, back))
+    blocks = jnp.stack([*lower[::-1], shard, *upper])
+    shift = lax.axis_index(axis) - len(lower)
+    blocks = blocks[(jnp.arange(peers) - shift) % peers]
+    return laid_out(blocks, dim)
 
 
 def partner(value, axis, bit):
@@ -40,7 +62,7 @@
     own_rank = lax.axis_index("expert")
     section_index = lax.axis_index("section")
     full_gate_up = lax.all_gather(gate_up, "dp", axis=3, tiled=True)
-    full_down = lax.all_gather(down_proj, "dp", axis=2, tiled=True)
+    full_down = collect(down_proj, "dp", 2)
     gate_weights = full_gate_up[0, 0, 0]
     up_weights = full_gate_up[0, 0, 1]
     down_weights = full_down[0, 0]

time: 781 us -> 742 us (0.950)
  waiting for transfers between devices: 627 us -> 561 us
  matrix products: 62.9 us -> 76 us
    all_gather x1 -> x0, waiting for transfers between devices: 49.1 us -> none  [per_device(): full_down = lax.all_gather(down_proj, 'dp', axis=2, tiled=True)]
    all_gather x2, waiting for transfers between devices: 259 us -> 210 us  [layer(): arrived = lax.all_gather(normed, 'expert', axis=0, tiled=True)]
    ppermute x0 -> x3, waiting for transfers between devices: none -> 34.6 us  [the longest x2 34.6 us: collect(): lower.append(lax.ppermute(lower[-1] if lower else shard, axis, pairs))]
    dot_general x2, matrix products: 23 us -> 52 us  [layer(): result = jnp.dot(active, down_weights, preferred_element_type=jnp.float32)]
    dot_general x2 -> x0, matrix products: 17.8 us -> none  [layer(): jnp.dot(arrived, gate_weights, preferred_element_type=jnp.float32)]
  transfers between devices with their start and end apart: 11 -> 13, of which waited for: 7 -> 7; matrix products, arithmetic and copies ran while one was open for 6% -> 9% of each run, Pallas kernels for 0% -> 0%
where the time goes in v1:
time: 742 us; the launch traced here: 741 us
  waiting for transfers between devices  561 us (76%)
  matrix products  76 us (10%)
  blocking collectives  32.8 us (4%)
  other arithmetic  29.7 us (4%)
  starting transfers between devices  15.7 us (2%)
  between operations  14 us (2%)
  local copies, waits for them, and re-layouts  11.9 us (2%)
    all_gather x2, waiting for transfers between devices, layer(): arrived = lax.all_gather(normed, 'expert', axis=0, tiled=True)  210 us
    reduce_scatter x2, waiting for transfers between devices, layer(): lax.psum_scatter(result, 'expert', scatter_dimension=0, tiled=True)  188 us
    all_gather x1, waiting for transfers between devices, per_device(): full_gate_up = lax.all_gather(gate_up, 'dp', axis=3, tiled=True)  117 us
    dot_general x2, matrix products, layer(): result = jnp.dot(active, down_weights, preferred_element_type=jnp.float32)  52 us
    ppermute x2, waiting for transfers between devices, collect(): lower.append(lax.ppermute(lower[-1] if lower else shard, axis, pairs))  34.6 us
    all_gather x1, blocking collectives, per_device(): all_mix = lax.all_gather(dense_mix, 'expert', axis=1, tiled=True)  32.8 us
    dot_general x2, matrix products, layer(): up_part = jnp.dot(arrived, up_weights, preferred_element_type=jnp.float32)  24.1 us
  transfers between devices with their start and end apart: 13, of which 7 were waited for; matrix products, arithmetic and copies ran while one was open for 9% of the time, Pallas kernels for 0%

profile of v1, /device:TPU:0, one launch (start us, length us, event | category | flops | bytes accessed | tf_op | source)
XLA Modules:
  0.0 741.5 jit_solution(15879222643350986988)
XLA Ops:
  9.5 1.7 fusion.8
  12.1 1.7 collective-permute-start
  13.8 1.6 collective-permute-start.2
  15.4 34.6 %collective-permute-done = bf16[1,1,192,4096]{3,2,1,0:T(8,128)(2,1)} collective-permute-done((bf16[1,1,192,4096]{3,2,1,0:T(8,128)(2,1)}, bf16[1,1,192,4096]{3,2,1,0:T(8,128)(2,1)}, u32[]{:S(2)}, u32[]{:S(2)}) %collective-permute-start) | collective-permute-done | bytes 1572896 | tf_op jit(solution)/shard_map/ppermute | solution.py:22
  50.2 3.9 collective-permute-start.4
  54.2 3.5 collective-permute-start.5
  57.8 32.8 %all_gather.14 = f32[2,1024,16]{2,0,1:T(2,128)S(1)} all-gather(f32[2,64,16]{2,0,1:T(2,128)S(1)} %copy.17), channel_id=1, replica_groups=mesh['section'=2,'expert'=16,'dp'=4] {'expert'}, dimensions={1}, use_global_device_ids=true | all-gather | bytes 139264 | tf_op jit(solution)/shard_map/all_gather | solution.py:74
  94.2 1.8 collective-permute-start.6
  96.0 6.6 maximum_bitcast_fusion
  102.5 6.4 gather_fusion
  108.9 137.7 %all-gather.4.cloned.1.call-done = bf16[1024,4096]{1,0:T(8,128)(2,1)} async-done(((bf16[64,4096]{1,0:T(8,128)(2,1)}), bf16[1024,4096]{1,0:T(8,128)(2,1)}) %all-gather.4.cloned.1.call-update) | async-done | bytes 8388624 | tf_op jit(solution)/shard_map/all_gather | solution.py:80
  246.6 117.1 %all-gather.6.cloned.1.call-done = bf16[1,1,2,4096,768]{4,3,2,1,0:T(8,128)(2,1)} async-done(((bf16[1,1,2,1024,768]{4,3,2,1,0:T(8,128)(2,1)}), bf16[1,1,2,4096,768]{4,3,2,1,0:T(8,128)(2,1)}) %all-gather.6.cloned.1.call-update) | async-done | bytes 12582928 | tf_op jit(solution)/shard_map/all_gather | solution.py:64
  363.7 12.0 %fusion.3 = f32[1024,768]{1,0:T(8,128)} fusion(bf16[1024,4096]{1,0:T(8,128)(2,1)} %all-gather.4.cloned.1.call-done, bf16[1,1,2,4096,768]{4,3,2,1,0:T(8,128)(2,1)} %all-gather.6.cloned.1.call-done), kind=kOutput, calls=%fused_computation.9 | convolution fusion | flops 6442450944 | bytes 17825792 | tf_op jit(solution)/shard_map/dot_general | solution.py:82
  375.7 26.0 %multiply_convert_fusion.1 = bf16[1024,4096]{1,0:T(8,128)(2,1)} fusion(f32[1024]{0:T(1024)S(1)} %bitcast.56, bf16[768,4096]{1,0:T(8,128)(2,1)} %bitcast.50, f32[1024,768]{1,0:T(8,128)} %fusion.3, bf16[1024,4096]{1,0:T(8,128)(2,1)} %all-gather.4.cloned.1.call-done, bf16[1,1,2,4096,768]{4,3,2,1,0:T(8,128)(2,1)} %all-gather.6.cloned.1.call-done), kind=kOutput, calls=%fused_computation.2 | convolution fusion | flops 12898009088 | bytes 32509952 | tf_op jit(solution)/shard_map/dot_general | solution.py:84
  401.9 103.5 %reduce-scatter.3.cloned.1.call-done = bf16[64,4096]{1,0:T(8,128)(2,1)} async-done(((bf16[1024,4096]{1,0:T(8,128)(2,1)}), bf16[64,4096]{1,0:T(8,128)(2,1)}) %reduce-scatter.3.cloned.1.call-update) | async-done | bytes 524304 | tf_op jit(solution)/shard_map/reduce_scatter | solution.py:88
  506.6 2.5 collective-permute-start.7
  509.1 10.1 %collective-permute-done.7 = bf16[64,4096]{1,0:T(8,128)(2,1)S(1)} collective-permute-done((bf16[64,4096]{1,0:T(8,128)(2,1)S(1)}, bf16[64,4096]{1,0:T(8,128)(2,1)S(1)}, u32[]{:S(2)}, u32[]{:S(2)}) %collective-permute-start.7) | collective-permute-done | bytes 524320 | tf_op jit(solution)/shard_map/ppermute | solution.py:38
  521.8 72.6 %all-gather.8.cloned.1.call-done = bf16[1024,4096]{1,0:T(8,128)(2,1)} async-done(((bf16[64,4096]{1,0:T(8,128)(2,1)}), bf16[1024,4096]{1,0:T(8,128)(2,1)}) %all-gather.8.cloned.1.call-update) | async-done | bytes 8388624 | tf_op jit(solution)/shard_map/all_gather | solution.py:80
  594.3 12.0 %fusion.2 = f32[1024,768]{1,0:T(8,128)} fusion(bf16[1024,4096]{1,0:T(8,128)(2,1)} %all-gather.8.cloned.1.call-done, bf16[1,1,2,4096,768]{4,3,2,1,0:T(8,128)(2,1)} %all-gather.6.cloned.1.call-done), kind=kOutput, calls=%fused_computation.8 | convolution fusion | flops 6442450944 | bytes 17825792 | tf_op jit(solution)/shard_map/dot_general | solution.py:82
  606.4 26.0 %multiply_convert_fusion = bf16[1024,4096]{1,0:T(8,128)(2,1)} fusion(f32[1024]{0:T(1024)S(1)} %bitcast.57, bf16[768,4096]{1,0:T(8,128)(2,1)} %bitcast.51, f32[1024,768]{1,0:T(8,128)} %fusion.2, bf16[1024,4096]{1,0:T(8,128)(2,1)} %all-gather.8.cloned.1.call-done, bf16[1,1,2,4096,768]{4,3,2,1,0:T(8,128)(2,1)} %all-gather.6.cloned.1.call-done), kind=kOutput, calls=%fused_computation.1 | convolution fusion | flops 12898009088 | bytes 32509952 | tf_op jit(solution)/shard_map/dot_general | solution.py:84
  634.2 4.8 broadcast_select_fusion
  639.1 3.7 broadcast_select_fusion.3
  642.8 5.0 broadcast_select_fusion.1
  647.7 84.9 %reduce-scatter.5.cloned.1.call-done = bf16[64,4096]{1,0:T(8,128)(2,1)} async-done(((bf16[1024,4096]{1,0:T(8,128)(2,1)}), bf16[64,4096]{1,0:T(8,128)(2,1)}) %reduce-scatter.5.cloned.1.call-update) | async-done | bytes 524304 | tf_op jit(solution)/shard_map/reduce_scatter | solution.py:88
  (72 shorter events, 15.0 us)
Async XLA Ops:
  7.2 47.0 %copy-start = (bf16[1,1,2,1024,768]{4,3,2,1,0:T(8,128)(2,1)S(1)}, bf16[1,1,2,1024,768]{4,3,2,1,0:T(8,128)(2,1)}, u32[]{:S(2)}) copy-start(bf16[1,1,2,1024,768]{4,3,2,1,0:T(8,128)(2,1)} %param.13) | copy-start | bytes 9437188
  7.2 50.5 %copy-start.14 = (f32[1,2,64,8]{2,3,1,0:T(8,128)S(1)}, f32[1,2,64,8]{2,3,1,0:T(8,128)}, u32[]{:S(2)}) copy-start(f32[1,2,64,8]{2,3,1,0:T(8,128)} %param.18) | copy-start | bytes 12292
  7.2 50.5 %copy-start.15 = (s32[1,2,64,8]{2,3,1,0:T(8,128)S(1)}, s32[1,2,64,8]{2,3,1,0:T(8,128)}, u32[]{:S(2)}) copy-start(s32[1,2,64,8]{2,3,1,0:T(8,128)} %param.17) | copy-start | bytes 12292
  7.2 239.4 %all-gather.4.cloned.1.call-start = ((), (), s32[]{:S(2)}) async-start(), calls=%async_computation.2 | async-start | bytes 8912896 | tf_op jit(solution)/shard_map/all_gather | solution.py:80
  11.3 352.4 %all-gather.6.cloned.1.call-start = ((), (), s32[]{:S(2)}) async-start(), calls=%async_computation.3 | async-start | bytes 15728640 | tf_op jit(solution)/shard_map/all_gather | solution.py:64
  12.0 493.4 %reduce-scatter.3.cloned.1.call-start = ((), (), s32[]{:S(2)}) async-start(), calls=%async_computation.4 | async-start | bytes 8912896 | tf_op jit(solution)/shard_map/reduce_scatter | solution.py:88
  12.1 37.9 %collective-permute-start = (bf16[1,1,192,4096]{3,2,1,0:T(8,128)(2,1)}, bf16[1,1,192,4096]{3,2,1,0:T(8,128)(2,1)}, u32[]{:S(2)}, u32[]{:S(2)}) collective-permute-start(bf16[1,1,192,4096]{3,2,1,0:T(8,128)(2,1)} %param.14), channel_id=1, source_target_pairs={{0,1},{1,2},{2,3},{3,0},{4,5},{5,6},{6,7},{7,4},{8,9},{9,10},{10,1... | collective-permute-start | bytes 4718600 | tf_op jit(solution)/shard_map/ppermute | solution.py:22
  13.8 80.4 %collective-permute-start.2 = (bf16[1,1,192,4096]{3,2,1,0:T(8,128)(2,1)}, bf16[1,1,192,4096]{3,2,1,0:T(8,128)(2,1)}, u32[]{:S(2)}, u32[]{:S(2)}) collective-permute-start(bf16[1,1,192,4096]{3,2,1,0:T(8,128)(2,1)} %param.14), channel_id=1, source_target_pairs={{1,0},{2,1},{3,2},{0,3},{5,4},{6,5},{7,6},{4,7},{9,8},{10,9},{11,1... | collective-permute-start | bytes 4718600 | tf_op jit(solution)/shard_map/ppermute | solution.py:24
  49.9 46.0 %collective-permute-start.1 = (bf16[1,1,192,4096]{3,2,1,0:T(8,128)(2,1)}, bf16[1,1,192,4096]{3,2,1,0:T(8,128)(2,1)}, u32[]{:S(2)}, u32[]{:S(2)}) collective-permute-start(bf16[1,1,192,4096]{3,2,1,0:T(8,128)(2,1)} %collective-permute-done), channel_id=1, source_target_pairs={{0,1},{1,2},{2,3},{3,0},{4,5},{5,6},{6,7},{7,4},{8,9},{9,10},{10,1... | collective-permute-start | bytes 4718600 | tf_op jit(solution)/shard_map/ppermute | solution.py:22
  50.2 351.5 %collective-permute-start.4 = (bf16[1,1,192,4096]{3,2,1,0:T(8,128)(2,1)}, bf16[1,1,192,4096]{3,2,1,0:T(8,128)(2,1)}, u32[]{:S(2)}, u32[]{:S(2)}) collective-permute-start(bf16[1,1,192,4096]{3,2,1,0:T(8,128)(2,1)} %param.14), channel_id=1, source_target_pairs={{0,32},{4,36},{8,40},{12,44},{16,48},{20,52},{24,56},{28,60},{32,0... | collective-permute-start | bytes 4718600 | tf_op jit(solution)/shard_map/ppermute | solution.py:32
  54.1 347.6 %collective-permute-start.3 = (bf16[1,1,2,1024,768]{4,3,2,1,0:T(8,128)(2,1)S(1)}, bf16[1,1,2,1024,768]{4,3,2,1,0:T(8,128)(2,1)}, u32[]{:S(2)}, u32[]{:S(2)}) collective-permute-start(bf16[1,1,2,1024,768]{4,3,2,1,0:T(8,128)(2,1)S(1)} %copy-done), channel_id=1, source_target_pairs={{0,32},{4,36},{8,40},{12,44},{16,48},{20,52},{24,56},{28,60},{32,0... | collective-permute-start | bytes 9437192 | tf_op jit(solution)/shard_map/ppermute | solution.py:32
  54.2 347.6 %collective-permute-start.5 = (bf16[1,1,192,4096]{3,2,1,0:T(8,128)(2,1)}, bf16[1,1,192,4096]{3,2,1,0:T(8,128)(2,1)}, u32[]{:S(2)}, u32[]{:S(2)}) collective-permute-start(bf16[1,1,192,4096]{3,2,1,0:T(8,128)(2,1)} %param.15), channel_id=1, source_target_pairs={{0,32},{4,36},{8,40},{12,44},{16,48},{20,52},{24,56},{28,60},{32,0... | collective-permute-start | bytes 4718600 | tf_op jit(solution)/shard_map/ppermute | solution.py:32
  94.2 307.6 %collective-permute-start.6 = (bf16[1,1,192,4096]{3,2,1,0:T(8,128)(2,1)}, bf16[1,1,192,4096]{3,2,1,0:T(8,128)(2,1)}, u32[]{:S(2)}, u32[]{:S(2)}) collective-permute-start(bf16[1,1,192,4096]{3,2,1,0:T(8,128)(2,1)} %param.16), channel_id=1, source_target_pairs={{0,32},{4,36},{8,40},{12,44},{16,48},{20,52},{24,56},{28,60},{32,0... | collective-permute-start | bytes 4718600 | tf_op jit(solution)/shard_map/ppermute | solution.py:32
  401.7 118.6 %copy-start.13 = (f32[1,4096]{1,0:T(1,128)S(1)}, f32[1,4096]{1,0:T(1,128)}, u32[]{:S(2)}) copy-start(f32[1,4096]{1,0:T(1,128)} %param.12) | copy-start | bytes 49156
  401.8 103.6 %copy-start.4 = (bf16[64,4096]{1,0:T(8,128)(2,1)S(1)}, bf16[64,4096]{1,0:T(8,128)(2,1)}, u32[]{:S(2)}) copy-start(bf16[64,4096]{1,0:T(8,128)(2,1)} %copy-done.3) | copy-start | bytes 1572868
  401.8 117.4 %copy-start.12 = (bf16[2,64,4096]{2,1,0:T(8,128)(2,1)S(1)}, bf16[2,64,4096]{2,1,0:T(8,128)(2,1)}, u32[]{:S(2)}) copy-start(bf16[2,64,4096]{2,1,0:T(8,128)(2,1)} %param.10) | copy-start | bytes 3145732
  401.8 119.8 %copy-start.9 = (f32[1,1024]{0,1:T(8,128)S(1)}, f32[1,1024]{0,1:T(8,128)}, u32[]{:S(2)}) copy-start(f32[1,1024]{0,1:T(8,128)} %get-tuple-element.20) | copy-start | bytes 12292
  401.8 192.5 %all-gather.8.cloned.1.call-start = ((), (), s32[]{:S(2)}) async-start(), calls=%async_computation.5 | async-start | bytes 8912896 | tf_op jit(solution)/shard_map/all_gather | solution.py:80
  506.6 12.6 %collective-permute-start.7 = (bf16[64,4096]{1,0:T(8,128)(2,1)S(1)}, bf16[64,4096]{1,0:T(8,128)(2,1)S(1)}, u32[]{:S(2)}, u32[]{:S(2)}) collective-permute-start(bf16[64,4096]{1,0:T(8,128)(2,1)S(1)} %fusion.9), channel_id=1, source_target_pairs={{0,64},{1,65},{2,66},{3,67},{4,68},{5,69},{6,70},{7,71},{8,72},{9,... | collective-permute-start | bytes 1572872 | tf_op jit(solution)/shard_map/ppermute | solution.py:38
  521.3 211.4 %reduce-scatter.5.cloned.1.call-start = ((), (), s32[]{:S(2)}) async-start(), calls=%async_computation.6 | async-start | bytes 8912896 | tf_op jit(solution)/shard_map/reduce_scatter | solution.py:88
  634.2 8.5 %copy-start.10 = (bf16[1,1,192,4096]{3,2,1,0:T(8,128)(2,1)S(1)}, bf16[1,1,192,4096]{3,2,1,0:T(8,128)(2,1)}, u32[]{:S(2)}) copy-start(bf16[1,1,192,4096]{3,2,1,0:T(8,128)(2,1)} %param.16) | copy-start | bytes 4718596
  634.2 8.5 %copy-start.11 = (bf16[1,1,192,4096]{3,2,1,0:T(8,128)(2,1)S(1)}, bf16[1,1,192,4096]{3,2,1,0:T(8,128)(2,1)}, u32[]{:S(2)}) copy-start(bf16[1,1,192,4096]{3,2,1,0:T(8,128)(2,1)} %param.15) | copy-start | bytes 4718596
  639.1 93.6 %copy-start.6 = (bf16[64,4096]{1,0:T(8,128)(2,1)S(1)}, bf16[64,4096]{1,0:T(8,128)(2,1)}, u32[]{:S(2)}) copy-start(bf16[64,4096]{1,0:T(8,128)(2,1)} %copy-done.5) | copy-start | bytes 1572868
  642.8 91.1 %copy-start.8 = (bf16[64,4096]{1,0:T(8,128)(2,1)S(1)}, bf16[64,4096]{1,0:T(8,128)(2,1)}, u32[]{:S(2)}) copy-start(bf16[64,4096]{1,0:T(8,128)(2,1)} %copy-done.7) | copy-start | bytes 1572868
  (6 other events, 12.7 us)
Sparse Core Ops, SparseCore 0:
  11.4 235.1 all-gather.3
  248.3 115.3 all-gather.5
  401.9 103.4 reduce-scatter.2
  521.4 72.8 all-gather.7
  632.5 100.1 reduce-scatter.4
